TPU v7x, 32 devices: a whole 2x2x4 slice. The times are simulated.
32 devices in a mesh: groups: 2 (over x), tgt: 16 (over z, y, core).
Axes of the slice: x: 2, y: 2, z: 4, core: 2. Of those that a mesh axis runs over, the one named last changes fastest.
Arguments:
- target_features: bfloat16 [32768, 1024], P(('groups', 'tgt')), parts along dimension 0, may hold values from -16 to 16
- source_features: bfloat16 [2048, 1024], P(('groups', 'tgt')), parts along dimension 0, may hold values from -16 to 16
- vectors: bfloat16 [2048, 128], P(('groups', 'tgt')), parts along dimension 0, may hold values from -6 to 6
- current: float32 [32768, 128], P(('groups', 'tgt')), parts along dimension 0, may hold values from -6 to 6
- previous: float32 [32768, 128], P(('groups', 'tgt')), parts along dimension 0, may hold values from -100 to 100
Outputs:
- filtered: float32 [32768, 128], P(('groups', 'tgt')), parts along dimension 0
There are 2 independent parts, one for each index of `groups`. A program takes and returns all parts, laid end to end along the dimension named above; each array names one. Nothing has to cross between parts.
All inputs are finite; a program needn't handle non-finite values.
Results may differ from a plain program's by a relative error of at most 0.002.
Values may be sent and summed in bfloat16 or wider, within the bound.
A program may use at most 128 MiB of HBM per device.

v0:
```python
import functools
import math

import jax
import jax.numpy as jnp
from jax import lax
from jax.experimental import pallas as pl
from jax.experimental.pallas import tpu as pltpu
from jax.sharding import PartitionSpec as P

MESH = pl.DeviceIdType.MESH
CORES = 2
PIECES = 2
TILE = 256
LANES = 128


def folded(mesh):
    line = mesh.devices.reshape(-1, mesh.shape["tgt"])[0][::CORES]
    spots = [getattr(device, "coords", None) for device in line]
    if None in spots or len(spots) % 2:
        return False
    moving = [axis for axis in range(3) if len({spot[axis] for spot in spots}) > 1]
    return len(moving) == 2 and any(len({spot[axis] for spot in spots}) == 2 for axis in moving)


def kernel(
    n, fold, target_hbm, source_hbm, vector_hbm, current_hbm, previous_hbm, next_hbm, scale_ref,
    target, current, previous, held, scores, top, result, column, local_sem, ring_send, ring_recv, pair_send, pair_recv,
    column_send, column_recv,
):
    me = lax.axis_index("tgt")
    chips = n // CORES
    last = chips // 2
    rows, depth = target_hbm.shape
    block = source_hbm.shape[0]
    part = block // PIECES
    gamma = 0.25 / math.sqrt(depth)
    core, chip = me % CORES, me // CORES

    def spot_of(c):
        if not fold:
            return c
        return (c % 2) * (chips - 1) + (c // 2) * (1 - 2 * (c % 2))

    def chip_at(spot):
        if not fold:
            return spot
        side = spot // last
        return (spot + side * (chips - 1 - 2 * spot)) * 2 + side

    spot = spot_of(chip)
    onward = chip_at((spot + chips + 1 - 2 * core) % chips) * CORES + core
    behind = chip_at((spot + chips - 1 + 2 * core) % chips) * CORES + core
    partner = chip * CORES + (1 - core)

    own = [
        pltpu.make_async_copy(source_hbm, held.at[pl.ds(0, block), pl.ds(0, depth)], local_sem.at[0]),
        pltpu.make_async_copy(vector_hbm, held.at[pl.ds(0, block), pl.ds(depth, LANES)], local_sem.at[1]),
    ]
    inputs = [
        pltpu.make_async_copy(target_hbm, target, local_sem.at[2]),
        pltpu.make_async_copy(current_hbm, current, local_sem.at[3]),
        pltpu.make_async_copy(previous_hbm, previous, local_sem.at[4]),
    ]
    for copy in own:
        copy.start()

    barrier = pltpu.get_barrier_semaphore()
    for other in (onward, behind, partner):
        pl.semaphore_signal(barrier, inc=1, device_id={"tgt": other}, device_id_type=MESH)
    pl.semaphore_wait(barrier, 3)

    def first_row(step):
        return 0 if step == 0 else CORES * block * (2 * step - 1)

    def pieces(step):
        return PIECES if step == last else CORES * PIECES

    def place(step, side, piece):
        side = side * (part if step == 0 else pieces(step) * part)
        return held.at[pl.ds(first_row(step) + side + piece * part, part)]

    sent = []

    def ring(step, piece):
        return pltpu.make_async_remote_copy(
            src_ref=place(step - 1, 0, piece),
            dst_ref=place(step, 0, piece),
            send_sem=ring_send.at[step - 1, piece],
            recv_sem=ring_recv.at[step - 1, piece],
            device_id={"tgt": onward},
            device_id_type=MESH,
        )

    def pair(step, piece):
        return pltpu.make_async_remote_copy(
            src_ref=place(step, 0, piece),
            dst_ref=place(step, PIECES if step == 0 else 1, piece),
            send_sem=pair_send.at[step, piece],
            recv_sem=pair_recv.at[step, piece],
            device_id={"tgt": partner},
            device_id_type=MESH,
        )

    def send(copy):
        copy.start()
        sent.append(copy)

    def settle(step):
        for piece in range(pieces(step)):
            pair(step, piece).wait_recv()

    for copy in own:
        copy.wait()
    for piece in range(PIECES):
        send(pair(0, piece))
        send(ring(1, piece))
    for piece in range(PIECES):
        pair(0, piece).wait_recv()
        send(ring(1, PIECES + piece))

    for copy in inputs:
        copy.start()
    top[...] = jnp.full_like(top, -jnp.inf)
    tiles = rows // TILE

    def squares(step):
        width = CORES * block * (2 if 0 < step < last else 1)
        at = pl.ds(first_row(step), width)
        feats = held[at, pl.ds(0, depth)].astype(jnp.float32)
        total = jnp.sum(feats * feats, axis=1, keepdims=True)
        return gamma * jnp.broadcast_to(total, (width, LANES)).T[0:1, :]

    def score(step, offset, low, high, height=TILE):
        width = CORES * block * (2 if 0 < step < last else 1)
        at = pl.ds(first_row(step), width)

        @pl.loop(low, high)
        def _(tile):
            span = pl.ds(pl.multiple_of(tile * height, height), height)
            dots = lax.dot_general(
                target[span, :], held[at, pl.ds(0, depth)], (((1,), (1,)), ((), ())),
                preferred_element_type=jnp.float32,
            )
            value = 2.0 * gamma * dots - offset
            scores[span, at] = value
            most = top[span, :]
            for lane in range(0, width, LANES):
                most = jnp.maximum(most, value[:, lane : lane + LANES])
            top[span, :] = most

    inputs[0].wait()
    score(0, squares(0), 0, tiles)
    for step in range(1, last + 1):
        if step > 1:
            settle(step - 1)
            offset = squares(step - 1)
        count = pieces(step)
        for piece in range(count):
            ring(step, piece).wait_recv()
            if step < last and piece < pieces(step + 1):
                send(ring(step + 1, piece))
            send(pair(step, piece))
            if step > 1:
                score(step - 1, offset, piece * tiles // count, (piece + 1) * tiles // count)
    settle(last)
    score(last, squares(last), 0, 1, rows)

    inputs[1].wait()
    inputs[2].wait()
    group = 2 * TILE

    def finish(tile, total):
        span = pl.ds(pl.multiple_of(tile * group, group), group)
        most = jnp.max(top[span, :], axis=1, keepdims=True)
        weights = jnp.exp(scores[span, :] - most)
        denominator = jnp.sum(weights, axis=1, keepdims=True)
        numer = jnp.dot(
            weights.astype(jnp.bfloat16), held[:, pl.ds(depth, LANES)], preferred_element_type=jnp.float32
        )
        value = 2.0 / 0.05 * (numer / denominator - 0.01 * current[span, :]) - previous[span, :]
        result[span, :] = value
        return total + jnp.sum((value * value).reshape(group // 8, 8, LANES), axis=0)

    total = lax.fori_loop(0, rows // group, finish, jnp.zeros((8, LANES), jnp.float32))
    column[0] = jnp.sum(total, axis=0, keepdims=True)
    output = pltpu.make_async_copy(result, next_hbm, local_sem.at[5])
    output.start()

    gifts = [
        pltpu.make_async_remote_copy(
            src_ref=column.at[0],
            dst_ref=column.at[gap],
            send_sem=column_send.at[gap],
            recv_sem=column_recv.at[gap],
            device_id={"tgt": (me + gap) % n},
            device_id_type=MESH,
        )
        for gap in range(1, n)
    ]
    for copy in gifts:
        copy.start()
    for copy in sent:
        copy.wait_send()
    for copy in gifts:
        copy.wait()
    scale_ref[...] = jnp.sqrt(jnp.sum(column[...], axis=0) / (rows * n) + 1e-06)
    output.wait()


def on_device(fold, target_features, source_features, vectors, current, previous):
    n = lax.axis_size("tgt")
    rows, depth = target_features.shape
    block, cols = vectors.shape
    steps = n // CORES // 2 + 1
    next_iter, scale = pl.pallas_call(
        functools.partial(kernel, n, fold),
        out_shape=(
            jax.ShapeDtypeStruct((rows, cols), jnp.float32),
            jax.ShapeDtypeStruct((1, cols), jnp.float32),
        ),
        in_specs=[pl.BlockSpec(memory_space=pl.ANY)] * 5,
        out_specs=[pl.BlockSpec(memory_space=pl.ANY), pl.BlockSpec(memory_space=pltpu.VMEM)],
        scratch_shapes=[
            pltpu.VMEM((rows, depth), jnp.bfloat16),
            pltpu.VMEM((rows, cols), jnp.float32),
            pltpu.VMEM((rows, cols), jnp.float32),
            pltpu.VMEM((n * block, depth + cols), jnp.bfloat16),
            pltpu.VMEM((rows, n * block), jnp.float32),
            pltpu.VMEM((rows, LANES), jnp.float32),
            pltpu.VMEM((rows, cols), jnp.float32),
            pltpu.VMEM((n, 1, cols), jnp.float32),
            pltpu.SemaphoreType.DMA((6,)),
            pltpu.SemaphoreType.DMA((steps, CORES * PIECES)),
            pltpu.SemaphoreType.DMA((steps, CORES * PIECES)),
            pltpu.SemaphoreType.DMA((steps, CORES * PIECES)),
            pltpu.SemaphoreType.DMA((steps, CORES * PIECES)),
            pltpu.SemaphoreType.DMA((n,)),
            pltpu.SemaphoreType.DMA((n,)),
        ],
        compiler_params=pltpu.CompilerParams(collective_id=0, has_side_effects=True),
    )(target_features, source_features, vectors, current, previous)
    return next_iter / scale


def solution(mesh):
    return jax.shard_map(
        functools.partial(on_device, folded(mesh)),
        mesh=mesh,
        in_specs=(P(("groups", "tgt"), None),) * 5,
        out_specs=P(("groups", "tgt"), None),
        check_vma=False,
    )
```

profile of v0, /device:TPU:0, one launch (start us, length us, event | category | flops | bytes accessed | tf_op | source)
XLA Modules:
  0.0 29.3 jit_solution(14253852203093447645)
XLA Ops:
  0.0 27.4 %shard_map.55 = (f32[1024,128]{1,0:T(8,128)}, f32[1,128]{1,0:T(1,128)}) custom-call(bf16[1024,1024]{1,0:T(8,128)(2,1)} %target_hbm.1, bf16[64,1024]{1,0:T(8,128)(2,1)} %source_hbm.1, bf16[64,128]{1,0:T(8,128)(2,1)} %vector_hbm.1, f32[1024,128]{1,0:T(8,128)} %current_hbm.1, f32[1024,128]{1,0:T(8,128)} %previous_hbm.1), custom_call_target="tpu_custom_call" | custom-call | tf_op jit(solution)/shard_map/pallas_call | solution.py:217
  27.4 1.9 %broadcast_divide_fusion = f32[1024,128]{1,0:T(8,128)} fusion(f32[1024,128]{1,0:T(8,128)} %get-tuple-element.7, f32[128]{0:T(128)} %bitcast.1), kind=kLoop, calls=%fused_computation | loop fusion | flops 131072 | bytes 1049088 | tf_op jit(solution)/shard_map/div | solution.py:244
where the time goes:
time: 29.4 us; the launch traced here: 29.3 us
  Pallas kernels  27.4 us (93%)
  other arithmetic  1.88 us (6%)
    pallas_call x1, Pallas kernels, on_device(): pl.pallas_call(functools.partial(kernel, n, fold), out_shape=(jax.ShapeDt...  27.4 us
    div x1, other arithmetic, on_device(): return next_iter / scale  1.88 us

commit v1 on v0

--- a/solution.py
+++ b/solution.py
@@ -25,8 +25,8 @@
 
 
 def kernel(
-    n, fold, target_hbm, source_hbm, vector_hbm, current_hbm, previous_hbm, next_hbm, scale_ref,
-    target, current, previous, held, scores, top, result, column, local_sem, ring_send, ring_recv, pair_send, pair_recv,
+    n, fold, target_hbm, source_hbm, vector_hbm, current_hbm, previous_hbm, result, scale_ref,
+    target, current, previous, held, scores, top, column, local_sem, ring_send, ring_recv, pair_send, pair_recv,
     column_send, column_recv,
 ):
     me = lax.axis_index("tgt")
@@ -185,8 +185,6 @@
 
     total = lax.fori_loop(0, rows // group, finish, jnp.zeros((8, LANES), jnp.float32))
     column[0] = jnp.sum(total, axis=0, keepdims=True)
-    output = pltpu.make_async_copy(result, next_hbm, local_sem.at[5])
-    output.start()
 
     gifts = [
         pltpu.make_async_remote_copy(
@@ -206,7 +204,6 @@
     for copy in gifts:
         copy.wait()
     scale_ref[...] = jnp.sqrt(jnp.sum(column[...], axis=0) / (rows * n) + 1e-06)
-    output.wait()
 
 
 def on_device(fold, target_features, source_features, vectors, current, previous):
@@ -217,11 +214,11 @@
     next_iter, scale = pl.pallas_call(
         functools.partial(kernel, n, fold),
         out_shape=(
-            jax.ShapeDtypeStruct((rows, cols), jnp.float32),
-            jax.ShapeDtypeStruct((1, cols), jnp.float32),
+            pltpu.VMEM((rows, cols), jnp.float32),
+            pltpu.VMEM((1, cols), jnp.float32),
         ),
         in_specs=[pl.BlockSpec(memory_space=pl.ANY)] * 5,
-        out_specs=[pl.BlockSpec(memory_space=pl.ANY), pl.BlockSpec(memory_space=pltpu.VMEM)],
+        out_specs=[pl.BlockSpec(memory_space=pltpu.VMEM)] * 2,
         scratch_shapes=[
             pltpu.VMEM((rows, depth), jnp.bfloat16),
             pltpu.VMEM((rows, cols), jnp.float32),
@@ -229,9 +226,8 @@
             pltpu.VMEM((n * block, depth + cols), jnp.bfloat16),
             pltpu.VMEM((rows, n * block), jnp.float32),
             pltpu.VMEM((rows, LANES), jnp.float32),
-            pltpu.VMEM((rows, cols), jnp.float32),
             pltpu.VMEM((n, 1, cols), jnp.float32),
-            pltpu.SemaphoreType.DMA((6,)),
+            pltpu.SemaphoreType.DMA((5,)),
             pltpu.SemaphoreType.DMA((steps, CORES * PIECES)),
             pltpu.SemaphoreType.DMA((steps, CORES * PIECES)),
             pltpu.SemaphoreType.DMA((steps, CORES * PIECES)),

time: 29.4 us -> 27.9 us (0.949)
  other arithmetic: 1.88 us -> 0.84 us
  Pallas kernels: 27.4 us -> 26.9 us
    div x1, other arithmetic: 1.88 us -> 0.84 us  [on_device(): return next_iter / scale]
    pallas_call x1, Pallas kernels: 27.4 us -> 26.9 us  [on_device(): pl.pallas_call(functools.partial(kernel, n, fold), out_shape=(pltpu.VMEM(...]
where the time goes in v1:
time: 27.9 us; the launch traced here: 27.7 us
  Pallas kernels  26.9 us (96%)
  other arithmetic  0.84 us (3%)
    pallas_call x1, Pallas kernels, on_device(): pl.pallas_call(functools.partial(kernel, n, fold), out_shape=(pltpu.VMEM(...  26.9 us
    div x1, other arithmetic, on_device(): return next_iter / scale  0.84 us

profile of v1, /device:TPU:0, one launch (start us, length us, event | category | flops | bytes accessed | tf_op | source)
XLA Modules:
  0.0 27.7 jit_solution(4616847557583197280)
XLA Ops:
  0.0 26.9 %shard_map.55 = (f32[1024,128]{1,0:T(8,128)S(1)}, f32[1,128]{1,0:T(1,128)S(1)}) custom-call(bf16[1024,1024]{1,0:T(8,128)(2,1)} %target_hbm.1, bf16[64,1024]{1,0:T(8,128)(2,1)} %source_hbm.1, bf16[64,128]{1,0:T(8,128)(2,1)} %vector_hbm.1, f32[1024,128]{1,0:T(8,128)} %current_hbm.1, f32[1024,128]{1,0:T(8,128)} %previous_hbm.1), custom_call_target="tpu_custom_call" | custom-call | tf_op jit(solution)/shard_map/pallas_call | solution.py:214
  26.9 0.8 %broadcast_divide_fusion = f32[1024,128]{1,0:T(8,128)} fusion(f32[1024,128]{1,0:T(8,128)S(1)} %get-tuple-element.7, f32[128]{0:T(128)S(1)} %bitcast.1), kind=kLoop, calls=%fused_computation | loop fusion | flops 131072 | bytes 1049088 | tf_op jit(solution)/shard_map/div | solution.py:240
